TPU v7x, 32 devices: a whole 2x2x4 slice. The times are simulated.
32 devices in a mesh: gx: 4 (over y, core), gy: 4 (over z), gz: 2 (over x).
Axes of the slice: x: 2, y: 2, z: 4, core: 2. Of those that a mesh axis runs over, the one named last changes fastest.
Arguments:
- stiffness: float32 [32, 48, 256], P('gx', 'gy', 'gz'), may hold values from 0.5 to 5
- density: float32 [32, 48, 256], P('gx', 'gy', 'gz'), may hold values from 1 to 4
- load: float32 [3, 32, 48, 256], P(None, 'gx', 'gy', 'gz'), may hold values from -6 to 6
- alive: int32 [4, 32, 48, 256], P(None, 'gx', 'gy', 'gz'), may hold values 0 or 1
- surf_coords: float32 [512, 3, 128], P(('gx', 'gy', 'gz')), may hold values from 0 to 1
- surf_nodes: int32 [512, 128], P(('gx', 'gy', 'gz')), may hold values from 0 to 12287
- routes: int32 [4, 512], P(None, ('gx', 'gy', 'gz')), may hold values from 0 to 1, as said below
- pairs: int32 [4, 32, 64, 2], P(None, ('gx', 'gy', 'gz')), may hold values from 0 to 15, as said below
Outputs:
- element_velocity: float32 [3, 32, 48, 256], P(None, 'gx', 'gy', 'gz')
- element_stress: float32 [6, 32, 48, 256], P(None, 'gx', 'gy', 'gz')
Inputs may be any that keep to these rules, and one draw needn't show every extreme that they name: `routes`: in every step a device sends at most 8 of its blocks to one box, and all devices of a gz column send exactly 8 blocks to one common box of that column. `pairs`: every slot named is live at that box and step whenever the box holds a block at all.
All inputs are finite; a program needn't handle non-finite values. No bound on the sum of `alive` on one device may be relied on, other than what follows from the above.
Results may differ from a plain program's by a relative error of at most 0.0003.
Values sent between devices are 32-bit elements; how exact they have to be, the bound alone decides.
A program may use at most 64 MiB of HBM per device.

v0:
```python
import functools
import math

import jax
import jax.numpy as jnp
from jax import lax
from jax.experimental import pallas as pl
from jax.experimental.pallas import tpu as pltpu
from jax.sharding import PartitionSpec as P

REPULSION = 1.0
KERNEL_SCALE = 0.08
TIME_STEP = 0.2
HIGHEST = lax.Precision.HIGHEST
MESH = pl.DeviceIdType.MESH
F32 = jnp.float32
BF16 = jnp.bfloat16
STRETCH = math.sqrt(math.log2(math.e) / KERNEL_SCALE)


def iota(shape, dim):
    return lax.broadcasted_iota(jnp.int32, shape, dim)


def hdot(a, b):
    return jnp.dot(a, b, preferred_element_type=F32, precision=HIGHEST)


def split2(x):
    high = x.astype(BF16)
    return high, (x - high.astype(F32)).astype(BF16)


def sum_x(q):
    return jnp.concatenate([q[:1], q[:-1] + q[1:], q[-1:]], axis=0)


def diff_x(q):
    return jnp.concatenate([-q[:1], q[:-1] - q[1:], q[-1:]], axis=0)


def body(sizes, stiff_hbm, dens_hbm, load_hbm, alive_hbm, coords_ref, nodes_ref, routes_ref, pairt_ref, pair_ref,
         vout_ref, sout_ref, *scratch):
    (stiff_ref, dens_ref, load_ref, alive_ref, in_sem, mod, big_f, rim_f, load_f, load_r, vel, vel_r, disp, disp_r, minv, minv_r, route_all, pos_all, slots, second,
     partial, send_f, ret, back_pick, rank_in, gather_w, lane_pick, lane_pick_h, touch, scatter_w, scatter_l,
     x_send, x_recv, y_send, y_recv, z_send, z_recv,
     route_ss, route_rs, pos_ss, pos_rs, ret_ss, ret_rs, x_ss, x_rs, y_ss, y_rs, z_ss, z_rs) = scratch
    count_x, count_y, cx, cy, cz, sb, npair, steps, nz, cap = sizes
    nx = cx + 1
    rows = 16
    ix, iy, iz = lax.axis_index("gx"), lax.axis_index("gy"), lax.axis_index("gz")
    lanes = iota((rows, cz), 1)
    lane3 = iota((1, 1, cz), 2)

    def roll(v, shift, axis):
        return pltpu.roll(v, shift % v.shape[axis], axis)

    inputs = [pltpu.make_async_copy(a, b, in_sem.at[k]) for k, (a, b) in enumerate((
        (stiff_hbm, stiff_ref), (alive_hbm, alive_ref), (load_hbm, load_ref), (dens_hbm, dens_ref)))]
    for c in inputs:
        c.start()

    for ref in (x_send, x_recv, y_send, y_recv, z_send, z_recv, mod, slots, send_f):
        ref[...] = jnp.zeros(ref.shape, ref.dtype)

    sides = (("gx", ix, count_x), ("gy", iy, count_y), ("gz", iz, nz))
    barrier = pltpu.get_barrier_semaphore()
    expect = jnp.int32(nz - 1)
    for name, at, count in sides[:2]:
        @pl.when(at > 0)
        def _():
            pl.semaphore_signal(barrier, inc=1, device_id={name: at - 1}, device_id_type=MESH)

        @pl.when(at < count - 1)
        def _():
            pl.semaphore_signal(barrier, inc=1, device_id={name: at + 1}, device_id_type=MESH)
        expect = expect + jnp.where(at > 0, 1, 0) + jnp.where(at < count - 1, 1, 0)
    for other in range(1, nz):
        pl.semaphore_signal(barrier, inc=1, device_id={"gz": lax.rem(iz + other, nz)}, device_id_type=MESH)
    pl.semaphore_wait(barrier, expect)

    def column(send_ref, recv_ref, ss, rs):
        out = []
        for other in range(1, nz):
            to = lax.rem(iz + other, nz)
            out.append(pltpu.make_async_remote_copy(
                src_ref=send_ref(to), dst_ref=recv_ref, send_sem=ss.at[other - 1], recv_sem=rs.at[other - 1],
                device_id={"gz": to}, device_id_type=MESH))
        return out

    def pos_copies(phase):
        return column(lambda to: pos_all.at[phase, iz], pos_all.at[phase, iz], pos_ss.at[phase], pos_rs.at[phase])

    def ret_copies(t):
        return column(lambda to: send_f.at[t, to], ret.at[t, iz], ret_ss.at[t], ret_rs.at[t])

    route_copies = column(lambda to: route_all.at[iz], route_all.at[iz], route_ss, route_rs)

    route_all[iz] = jnp.full((8, 128), -1, jnp.int32)
    route_all[iz, 0:steps, 0:sb] = routes_ref[...]
    for x in range(3):
        pos_all[0, iz, :, x * 128:(x + 1) * 128] = coords_ref[x]
    for c in route_copies + pos_copies(0):
        c.start()

    for c in inputs:
        c.wait()
    for t in range(steps):
        for i in range(cx):
            mod[t, i, 0:cy, :] = stiff_ref[:, i, :] * alive_ref[t, :, i, :].astype(F32)
    for c in range(4):
        for i in range(cx):
            mod[steps + c, i, 0:cy, :] = 0.125 * (load_ref[c, :, i, :] if c < 3 else dens_ref[:, i, :])
    rim = jnp.zeros((rows, cz), F32)
    for c in range(4):
        q = sum_x(mod[steps + c])
        q = q + roll(q, 1, 1)
        r = roll(q, 1, 2)
        load_f[c] = q + jnp.where(lane3 > 0, r, 0.0)
        for i in range(nx):
            at = c * nx + i
            rim = rim + jnp.where(lanes == at, roll(r[i], at, 1), 0.0)
    load_r[...] = rim

    ids = nodes_ref[...]
    row = lax.shift_right_logical(ids, jnp.full(ids.shape, cz.bit_length() - 1, jnp.int32))
    lane = ids & (cz - 1)
    wide = row
    for m in range(1, cx):
        wide = wide + jnp.where(row >= cy * m, rows - cy, 0)
    depth = cx * rows
    wide_pad = jnp.concatenate([wide.astype(F32), jnp.zeros((128 - sb, 128), F32)], axis=0)
    wide_t = jnp.transpose(wide_pad)
    for s in range(sb):
        hot = (iota((depth, 128), 0) == wide[s:s + 1, :]).astype(F32).astype(BF16)
        gather_w[s, 0:depth, :] = hot
        gather_w[s, depth:2 * depth, :] = hot
        pick = (iota((cz, 128), 0) == lane[s:s + 1, :]).astype(F32)
        lane_pick[s] = pick
        lane_pick_h[s] = pick.astype(BF16)
        col = jnp.broadcast_to(wide_t[:, s:s + 1], (128, depth))
        hot = (iota((128, depth), 1).astype(F32) == col).astype(F32).astype(BF16)
        scatter_w[s * 256:s * 256 + 128, :] = hot
        scatter_w[s * 256 + 128:s * 256 + 256, :] = hot

    def wait_all(copies):
        for c in copies:
            c.wait()

    wait_all(route_copies)
    upper = (iota((128, 128), 0) <= iota((128, 128), 1)).astype(F32)
    own = route_all[iz]
    for b in range(nz):
        hits = (route_all[b] == iz).astype(F32)
        rank_in[b] = jnp.where(hits > 0, jnp.dot(hits, upper, preferred_element_type=F32), 0.0)
    slot8 = nz * 8
    picks = []
    for b in range(nz):
        hits = (own == b).astype(F32)
        picks.append(jnp.where(hits > 0, jnp.dot(hits, upper, preferred_element_type=F32), 0.0))
    ranks8 = (iota((8, 128), 0) + 1).astype(F32)
    live8 = iota((8, 128), 0) < cap
    for t in range(steps):
        parts = [jnp.where((picks[b][t:t + 1, :] == ranks8) & live8, 1.0, 0.0) for b in range(nz)]
        table = jnp.concatenate(parts + [jnp.zeros((128 - slot8, 128), F32)], axis=0)
        back_pick[t] = jnp.transpose(table)[0:sb, :]

    def gather(phase):
        highs, lows = [], []
        for c in range(3):
            flat = jnp.transpose(disp[c, 0:cx].reshape(depth, cz))
            high, low = split2(flat)
            highs.append(high)
            lows.append(low)
        left = jnp.concatenate([jnp.concatenate(highs, axis=0), jnp.concatenate(lows, axis=0)], axis=1)
        for s in range(0, sb, 2):
            got = jnp.dot(left, jnp.concatenate([gather_w[s], gather_w[s + 1]], axis=1), preferred_element_type=F32)
            for h in range(2):
                for c in range(3):
                    part = got[c * cz:(c + 1) * cz, h * 128:(h + 1) * 128] * lane_pick[s + h]
                    pos_all[phase, iz, s + h:s + h + 1, c * 128:(c + 1) * 128] = (
                        jnp.sum(part, axis=0, keepdims=True) + coords_ref[c, s + h:s + h + 1, :])

    def build_slots(t, phase):
        live = []
        for b in range(nz):
            hot = jnp.where(rank_in[b, t:t + 1, :] == ranks8[0:cap], 1.0, 0.0)
            live.append(jnp.sum(hot, axis=1, keepdims=True))
            got = STRETCH * hdot(hot[:, 0:sb], pos_all[phase, b])
            for x in range(3):
                slots[x, b * cap:(b + 1) * cap, :] = got[:, x * 128:(x + 1) * 128]
        for x in range(3):
            flipped = jnp.transpose(slots[x])
            for k in range(nz * cap):
                second[k, x] = jnp.broadcast_to(flipped[:, k:k + 1], (128, 128))
        return live

    unroll = 4

    def pair_range(t, start, stop):
        def some(at, carry):
            for u in range(unroll):
                one(start + at * unroll + u)
            return carry

        def one(q):
            p = pair_ref[t, 0, q]
            r = pair_ref[t, 1, q]
            xi = [jnp.broadcast_to(slots[x, pl.ds(p, 1), :], (8, 128)) for x in range(3)]
            acc = [jnp.zeros((8, 128), F32)] * 3
            for j in range(16):
                d = [xi[x] - second[r, x, j * 8:(j + 1) * 8, :] for x in range(3)]
                w = jnp.exp2(-(d[0] * d[0] + d[1] * d[1] + d[2] * d[2]))
                acc = [acc[x] + d[x] * w for x in range(3)]
            for x in range(3):
                partial[x, pl.ds(q, 1), :] = jnp.sum(acc[x], axis=0, keepdims=True)
        lax.fori_loop(0, (stop - start) // unroll, some, 0)

    def finish_pairs(t, live):
        first = pairt_ref[t, 0:1, :]
        other = pairt_ref[t, 1:2, :]
        live_p = jnp.zeros((1, npair), F32)
        live_r = jnp.zeros((1, npair), F32)
        for b in range(nz):
            slot = iota((cap, npair), 0) + b * cap
            live_p = live_p + jnp.sum(jnp.where(first == slot, live[b], 0.0), axis=0, keepdims=True)
            live_r = live_r + jnp.sum(jnp.where(other == slot, live[b], 0.0), axis=0, keepdims=True)
        weight = live_p * live_r * (REPULSION / STRETCH)
        for b in range(nz):
            hot = jnp.where(first == iota((cap, npair), 0) + b * cap, weight, 0.0)
            for x in range(3):
                send_f[t, b, 0:cap, x * 128:(x + 1) * 128] = hdot(hot, partial[x])
        for c in ret_copies(t):
            c.start()
        ret[t, iz] = send_f[t, iz]

    def scatter(t):
        wait_all(ret_copies(t))
        force = hdot(back_pick[t, :, 0:slot8], ret[t].reshape(slot8, 384))
        for c in range(3):
            for s in range(sb):
                line = jnp.broadcast_to(force[s:s + 1, c * 128:(c + 1) * 128], (16, 128))
                for h, half in enumerate(split2(line)):
                    spread = lane_pick_h[s].reshape(cz // 16, 16, 128) * half[None]
                    scatter_l[2 * s + h, c * cz:(c + 1) * cz, :] = spread.reshape(cz, 128)
        left = jnp.concatenate([scatter_l[k] for k in range(2 * sb)], axis=1)
        total = jnp.dot(left, scatter_w[...], preferred_element_type=F32)
        for c in range(3):
            grid = jnp.transpose(total[c * cz:(c + 1) * cz, :]).reshape(cx, rows, cz)
            touch[c] = grid

    def corners(field, rim_value, c):
        u = field[c]
        edge = jnp.stack([roll(rim_value, -(c * nx + i), 1) for i in range(nx)])
        above = roll(jnp.where(lane3 == 0, edge, u), -1, 2)
        both = u + above
        step = above - u
        shifted = roll(both, -1, 1)
        return both + shifted, shifted - both, step + roll(step, -1, 1)

    def stress_of(modulus):
        grads = []
        rim_value = disp_r[...]
        for c in range(3):
            mean, along_y, along_z = corners(disp, rim_value, c)
            grads.append((0.25 * (mean[1:] - mean[:-1]), 0.25 * (along_y[1:] + along_y[:-1]),
                          0.25 * (along_z[1:] + along_z[:-1])))
        trace = grads[0][0] + grads[1][1] + grads[2][2]
        return (modulus * (2.0 * grads[0][0] + trace), modulus * (2.0 * grads[1][1] + trace),
                modulus * (2.0 * grads[2][2] + trace), modulus * (grads[0][1] + grads[1][0]),
                modulus * (grads[1][2] + grads[2][1]), modulus * (grads[0][2] + grads[2][0]))

    def internal(t):
        s = stress_of(mod[t])
        table = ((s[0], s[3], s[5]), (s[3], s[1], s[4]), (s[5], s[4], s[2]))
        rim = load_r[...]
        for c in range(3):
            a0 = -0.25 * diff_x(table[c][0])
            ay = -0.25 * sum_x(table[c][1])
            az = -0.25 * sum_x(table[c][2])
            a = (a0 - ay) + roll(a0 + ay, 1, 1)
            b = az + roll(az, 1, 1)
            r = roll(a + b, 1, 2)
            big_f[c] = load_f[c] + (a - b) + jnp.where(lane3 > 0, r, 0.0)
            for i in range(nx):
                at = c * nx + i
                rim = rim + jnp.where(lanes == at, roll(r[i], at, 1), 0.0)
        rim_f[...] = rim

    def axis_copies(side, send, recv, ss, rs, t, used):
        name, at, count = side
        out = []
        for way, to, sends, gets in ((0, at - 1, at > 0, at < count - 1), (1, at + 1, at < count - 1, at > 0)):
            out.append((pltpu.make_async_remote_copy(
                src_ref=send.at[t, way, 0:used], dst_ref=recv.at[t, way, 0:used], send_sem=ss.at[t, way],
                recv_sem=rs.at[t, way], device_id={name: to}, device_id_type=MESH), sends, gets))
        return out

    def start(copies):
        for copy, sends, _ in copies:
            @pl.when(sends)
            def _():
                copy.start()

    def finish(copies):
        for copy, sends, gets in copies:
            @pl.when(sends)
            def _():
                copy.wait_send()

            @pl.when(gets)
            def _():
                copy.wait_recv()

    def halo(t, fillers):
        comps = 4 if t == 0 else 3
        low_lane = functools.reduce(jnp.logical_or, [lanes == c * nx for c in range(4)])
        high_lane = functools.reduce(jnp.logical_or, [lanes == c * nx + cx for c in range(4)])
        for way, plane in ((0, 0), (1, cx)):
            x_send[t, way, 0] = rim_f[...]
            for c in range(comps):
                x_send[t, way, 1 + c] = big_f[c, plane]
        copies = axis_copies(sides[0], x_send, x_recv, x_ss, x_rs, t, comps + 1)
        start(copies)
        fillers[0]()
        finish(copies)
        for c in range(comps):
            big_f[c, 0] = big_f[c, 0] + x_recv[t, 1, 1 + c]
            big_f[c, cx] = big_f[c, cx] + x_recv[t, 0, 1 + c]
        rim_f[...] = (rim_f[...] + jnp.where(low_lane, roll(x_recv[t, 1, 0], -cx, 1), 0.0)
                      + jnp.where(high_lane, roll(x_recv[t, 0, 0], cx, 1), 0.0))

        used = -(-(1 + comps * nx) // 8) * 8
        for way, line in ((0, 0), (1, cy)):
            y_send[t, way, 0:1] = rim_f[line:line + 1]
            for c in range(comps):
                for i in range(nx):
                    at = 1 + c * nx + i
                    y_send[t, way, at:at + 1] = big_f[c, i, line:line + 1]
        copies = axis_copies(sides[1], y_send, y_recv, y_ss, y_rs, t, used)
        start(copies)
        fillers[1]()
        finish(copies)
        for way, line in ((1, 0), (0, cy)):
            rim_f[line:line + 1] = rim_f[line:line + 1] + y_recv[t, way, 0:1]
            for c in range(comps):
                for i in range(nx):
                    at = 1 + c * nx + i
                    big_f[c, i, line:line + 1] = big_f[c, i, line:line + 1] + y_recv[t, way, at:at + 1]

        packed = jnp.zeros((rows, cz), F32)
        for c in range(comps):
            for i in range(nx):
                at = c * nx + i
                packed = jnp.where(lanes == at, roll(big_f[c, i], at, 1), packed)
        z_send[t, 0] = packed
        z_send[t, 1] = rim_f[...]
        copies = axis_copies(sides[2], z_send, z_recv, z_ss, z_rs, t, rows)
        start(copies)
        fillers[2]()
        finish(copies)
        rim_f[...] = rim_f[...] + z_recv[t, 0]
        below = z_recv[t, 1]
        for c in range(comps):
            for i in range(nx):
                at = c * nx + i
                big_f[c, i] = big_f[c, i] + jnp.where(lanes == 0, roll(below, -at, 1), 0.0)

    def contact(t, phase):
        cut = npair // (3 if phase > 0 else 2) // unroll * unroll
        held = []

        def first():
            if phase > 0:
                wait_all(pos_copies(phase))
                held.append(build_slots(t, phase))
            else:
                held.append(early)
            pair_range(t, 0, cut)

        def middle():
            pair_range(t, cut, npair)
            finish_pairs(t, held[0])

        return [first, middle, lambda: scatter(t)]

    wait_all(pos_copies(0))
    live = build_slots(0, 0)
    pair_range(0, 0, npair)
    finish_pairs(0, live)
    early = build_slots(1, 0)
    scatter(0)

    for t in range(steps):
        if t == 0:
            big_f[...] = load_f[...]
            rim_f[...] = load_r[...]
        else:
            if t + 1 < steps:
                gather(t)
                for c in pos_copies(t):
                    c.start()
            internal(t)
        for c in range(3):
            big_f[c, 0:cx] = big_f[c, 0:cx] + touch[c]
        halo(t, contact(t + 1, t) if t + 1 < steps else [lambda: None] * 3)
        if t == 0:
            mass = big_f[3]
            minv[...] = jnp.where(mass > 0.0, 1.0 / mass, 0.0)
            held = jnp.where((lanes >= 3 * nx) & (lanes < 4 * nx), rim_f[...], 0.0)
            spread = roll(held, -3 * nx, 1) + roll(held, -2 * nx, 1) + roll(held, -nx, 1)
            minv_r[...] = jnp.where(spread > 0.0, 1.0 / spread, 0.0)
            for c in range(3):
                vel[c] = TIME_STEP * (big_f[c] * minv[...])
            vel_r[...] = TIME_STEP * (rim_f[...] * minv_r[...])
            disp[...] = TIME_STEP * vel[...]
            disp_r[...] = TIME_STEP * vel_r[...]
        else:
            for c in range(3):
                vel[c] = vel[c] + TIME_STEP * (big_f[c] * minv[...])
            vel_r[...] = vel_r[...] + TIME_STEP * (rim_f[...] * minv_r[...])
            disp[...] = disp[...] + TIME_STEP * vel[...]
            disp_r[...] = disp_r[...] + TIME_STEP * vel_r[...]

    rim_value = vel_r[...]
    for c in range(3):
        mean, _, _ = corners(vel, rim_value, c)
        mean = 0.125 * (mean[1:] + mean[:-1])
        for i in range(cx):
            vout_ref[c, :, i, :] = mean[i, 0:cy, :]
    s = stress_of(mod[steps - 1])
    for c in range(6):
        for i in range(cx):
            sout_ref[c, :, i, :] = s[c][i, 0:cy, :]


def per_device(stiffness, density, load, alive, surf_coords, surf_nodes, routes, pairs):
    cx, cy, cz = stiffness.shape
    steps = alive.shape[0]
    sb = surf_coords.shape[0]
    npair = pairs.shape[2]
    count_x, count_y, nz = (lax.axis_size(a) for a in ("gx", "gy", "gz"))
    cap = max(sb // 4, sb // nz)
    nx = cx + 1
    pairt = jnp.transpose(pairs[:, 0], (0, 2, 1))
    sizes = (count_x, count_y, cx, cy, cz, sb, npair, steps, nz, cap)
    vm = lambda *shape: pltpu.VMEM(shape, F32)
    dma = lambda *shape: pltpu.SemaphoreType.DMA(shape)
    column = max(nz - 1, 1)
    scratch = [
        vm(cy, cx, cz), vm(cy, cx, cz), vm(3, cy, cx, cz), pltpu.VMEM((steps, cy, cx, cz), jnp.int32), dma(4),
        vm(steps + 4, cx, 16, cz), vm(4, nx, 16, cz), vm(16, cz), vm(4, nx, 16, cz), vm(16, cz),
        vm(3, nx, 16, cz), vm(16, cz), vm(3, nx, 16, cz), vm(16, cz), vm(nx, 16, cz), vm(16, cz),
        pltpu.VMEM((nz, 8, 128), jnp.int32), vm(steps - 1, nz, sb, 384), vm(3, 128, 128), vm(nz * cap, 3, 128, 128),
        vm(3, npair, 128), vm(steps, nz, 8, 384), vm(steps, nz, 8, 384), vm(steps, sb, 128), vm(nz, 8, 128),
        pltpu.VMEM((sb, 2 * cx * 16, 128), BF16), vm(sb, cz, 128), pltpu.VMEM((sb, cz, 128), BF16),
        vm(3, cx, 16, cz), pltpu.VMEM((2 * sb * 128, cx * 16), BF16),
        pltpu.VMEM((2 * sb, 3 * cz, 128), BF16),
        vm(steps, 2, 5, 16, cz), vm(steps, 2, 5, 16, cz), vm(steps, 2, 40, cz), vm(steps, 2, 40, cz),
        vm(steps, 2, 16, cz), vm(steps, 2, 16, cz),
        dma(column), dma(column), dma(steps - 1, column), dma(steps - 1, column), dma(steps, column), dma(steps, column),
        dma(steps, 2), dma(steps, 2), dma(steps, 2), dma(steps, 2), dma(steps, 2), dma(steps, 2),
    ]
    vmem = pl.BlockSpec(memory_space=pltpu.VMEM)
    vel, stress = pl.pallas_call(
        functools.partial(body, sizes),
        out_shape=(jax.ShapeDtypeStruct((3, cy, cx, cz), F32), jax.ShapeDtypeStruct((6, cy, cx, cz), F32)),
        in_specs=[pl.BlockSpec(memory_space=pltpu.MemorySpace.HBM)] * 4 + [vmem] * 4 + [pl.BlockSpec(memory_space=pltpu.SMEM)],
        out_specs=(vmem, vmem),
        scratch_shapes=scratch,
        compiler_params=pltpu.CompilerParams(collective_id=0, has_side_effects=True, vmem_limit_bytes=56 * 1024 * 1024),
    )(jnp.swapaxes(stiffness, 0, 1), jnp.swapaxes(density, 0, 1), jnp.swapaxes(load, 1, 2), jnp.swapaxes(alive, 1, 2),
      jnp.swapaxes(surf_coords, 0, 1), surf_nodes, routes, pairt, pairt)
    return jnp.swapaxes(vel, 1, 2), jnp.swapaxes(stress, 1, 2)


def solution(mesh):
    return jax.shard_map(
        per_device,
        mesh=mesh,
        in_specs=(
            P("gx", "gy", "gz"),
            P("gx", "gy", "gz"),
            P(None, "gx", "gy", "gz"),
            P(None, "gx", "gy", "gz"),
            P(("gx", "gy", "gz"), None, None),
            P(("gx", "gy", "gz"), None),
            P(None, ("gx", "gy", "gz")),
            P(None, ("gx", "gy", "gz"), None, None),
        ),
        out_specs=(P(None, "gx", "gy", "gz"), P(None, "gx", "gy", "gz")),
        check_vma=False,
    )
```

profile of v0, /device:TPU:1, one launch (start us, length us, event | category | flops | bytes accessed | tf_op | source)
XLA Modules:
  0.0 62.1 jit_solution(18136510381899425417)
XLA Ops:
  0.6 59.1 %shard_map.95 = (f32[3,12,8,128]{3,2,1,0:T(8,128)}, f32[6,12,8,128]{3,2,1,0:T(8,128)}) custom-call(f32[12,8,128]{2,1,0:T(8,128)} %bitcast.14, f32[12,8,128]{2,1,0:T(8,128)} %bitcast.15, f32[3,12,8,128]{3,2,1,0:T(8,128)} %bitcast.13, s32[4,12,8,128]{3,2,1,0:T(8,128)} %bitcast.11, f32[3,16,128]{2,1,0:T(8,128)} %bitcast.16, s32[16,128]{1,0:T(8,128)} %nodes_ref.1, ...), custom_call_target="tpu_custom_call" | custom-call | tf_op jit(solution)/shard_map/pallas_call | solution.py:465
  59.8 0.0 copy-start
  59.8 1.6 %copy.12 = f32[3,8,12,128]{3,1,2,0:T(8,128)} copy(f32[3,8,12,128]{3,1,2,0:T(8,128)} %bitcast.12) | data formatting | bytes 294912
  61.4 0.0 copy-done
  61.4 0.7 %copy.13 = f32[6,8,12,128]{3,1,2,0:T(8,128)} copy(f32[6,8,12,128]{3,1,2,0:T(8,128)S(1)} %bitcast.10) | data formatting | bytes 589824
Async XLA Ops:
  59.8 1.6 %copy-start = (f32[6,12,8,128]{3,2,1,0:T(8,128)S(1)}, f32[6,12,8,128]{3,2,1,0:T(8,128)}, u32[]{:S(2)}) copy-start(f32[6,12,8,128]{3,2,1,0:T(8,128)} %get-tuple-element.5) | copy-start | bytes 884740
where the time goes:
time: 62.4 us; the launch traced here: 62.1 us
  Pallas kernels  59.1 us (95%)
  local copies, waits for them, and re-layouts  2.34 us (4%)
  between operations  0.65 us (1%)
    pallas_call x1, Pallas kernels, per_device(): pl.pallas_call(functools.partial(body, sizes), out_shape=(jax.ShapeDtypeS...  59.1 us
    unnamed x4, local copies, waits for them, and re-layouts  2.34 us

commit v1 on v0

v1 whole, which is shorter than its diff:
```python
import functools
import itertools
import math

import jax
import jax.numpy as jnp
from jax import lax
from jax.experimental import pallas as pl
from jax.experimental.pallas import tpu as pltpu
from jax.sharding import PartitionSpec as P

REPULSION = 1.0
KERNEL_SCALE = 0.08
TIME_STEP = 0.2
HIGHEST = lax.Precision.HIGHEST
MESH = pl.DeviceIdType.MESH
F32 = jnp.float32
BF16 = jnp.bfloat16
STRETCH = math.sqrt(2.0 * math.log2(math.e) / KERNEL_SCALE)
FEATURES = 32
UNROLL = 16


def iota(shape, dim):
    return lax.broadcasted_iota(jnp.int32, shape, dim)


def hdot(a, b):
    return jnp.dot(a, b, preferred_element_type=F32, precision=HIGHEST)


def split2(x):
    high = x.astype(BF16)
    return high, (x - high.astype(F32)).astype(BF16)


def split3(x):
    high = x.astype(BF16).astype(F32)
    rest = x - high
    middle = rest.astype(BF16).astype(F32)
    return high, middle, rest - middle


def bdot(a, b):
    return jnp.dot(a, b, preferred_element_type=F32)


def sum_x(q):
    return jnp.concatenate([q[:1], q[:-1] + q[1:], q[-1:]], axis=0)


def diff_x(q):
    return jnp.concatenate([-q[:1], q[:-1] - q[1:], q[-1:]], axis=0)


def body(sizes, stiff_hbm, dens_hbm, load_hbm, alive_hbm, coords_ref, nodes_ref, routes_ref, pairt_ref, pair_ref,
         vout_ref, sout_ref, *scratch):
    (stiff_ref, dens_ref, load_ref, alive_ref, in_sem, mod, big_f, rim_f, load_f, load_r, vel, vel_r, disp, disp_r, minv, minv_r, route_all, pos_all, slots, feat_a, feat_b, take_a, turned_b, give_b,
     partial, send_f, ret, back_pick, choose, pair_hot, rank_in, row_pick, lane_pick, lane_turn, flat, touch, scatter_l,
     x_send, x_recv, y_send, y_recv, edge_send, edge_recv, z_send, z_recv, zx_recv, line_send, line_recv,
     route_ss, route_rs, pos_ss, pos_rs, ret_ss, ret_rs, halo_ss, halo_rs) = scratch
    count_x, count_y, cx, cy, cz, sb, npair, steps, nz, cap = sizes
    nx = cx + 1
    rows = 16
    nslots = nz * cap
    ix, iy, iz = lax.axis_index("gx"), lax.axis_index("gy"), lax.axis_index("gz")
    lanes = iota((rows, cz), 1)
    lane3 = iota((1, 1, cz), 2)

    def roll(v, shift, axis):
        return pltpu.roll(v, shift % v.shape[axis], axis)

    inputs = [pltpu.make_async_copy(a, b, in_sem.at[k]) for k, (a, b) in enumerate((
        (stiff_hbm, stiff_ref), (alive_hbm, alive_ref), (load_hbm, load_ref), (dens_hbm, dens_ref)))]
    for c in inputs:
        c.start()

    for ref in (x_recv, y_send, y_recv, edge_recv, z_recv, zx_recv, line_recv, mod, feat_a, feat_b, send_f):
        ref[...] = jnp.zeros(ref.shape, ref.dtype)

    sides = (("gx", ix, count_x), ("gy", iy, count_y), ("gz", iz, nz))
    ways = sorted((d for d in itertools.product((-1, 0, 1), repeat=3) if any(d)), key=lambda d: (-abs(d[2]), -sum(map(abs, d))))

    def there(d, sign):
        return functools.reduce(jnp.logical_and, [
            (at + sign * step >= 0) & (at + sign * step < count) for step, (_, at, count) in zip(d, sides) if step])

    def neighbor(d):
        return {name: at + step for step, (name, at, _) in zip(d, sides) if step}

    sends = [there(d, 1) for d in ways]
    gets = [there(d, -1) for d in ways]
    barrier = pltpu.get_barrier_semaphore()
    expect = jnp.int32(0)
    for d, here in zip(ways, sends):
        @pl.when(here)
        def _():
            pl.semaphore_signal(barrier, inc=1, device_id=neighbor(d), device_id_type=MESH)
        expect = expect + jnp.where(here, 1, 0)
    for other in (range(1, nz) if nz > 2 else ()):
        far = lax.rem(iz + other, nz)
        apart = jnp.logical_and(far != iz - 1, far != iz + 1)

        @pl.when(apart)
        def _():
            pl.semaphore_signal(barrier, inc=1, device_id={"gz": far}, device_id_type=MESH)
        expect = expect + jnp.where(apart, 1, 0)
    pl.semaphore_wait(barrier, expect)

    def column(send_ref, recv_ref, ss, rs):
        out = []
        for other in range(1, nz):
            to = lax.rem(iz + other, nz)
            out.append(pltpu.make_async_remote_copy(
                src_ref=send_ref(to), dst_ref=recv_ref, send_sem=ss.at[other - 1], recv_sem=rs.at[other - 1],
                device_id={"gz": to}, device_id_type=MESH))
        return out

    def pos_copies(phase):
        return column(lambda to: pos_all.at[phase, iz], pos_all.at[phase, iz], pos_ss.at[phase], pos_rs.at[phase])

    def ret_copies(t):
        return column(lambda to: send_f.at[t, to], ret.at[t, iz], ret_ss.at[t], ret_rs.at[t])

    route_copies = column(lambda to: route_all.at[iz], route_all.at[iz], route_ss, route_rs)

    route_all[iz] = jnp.full((8, 128), -1, jnp.int32)
    route_all[iz, 0:steps, 0:sb] = routes_ref[...]
    for x in range(3):
        pos_all[0, iz, :, x * 128:(x + 1) * 128] = coords_ref[x]
    for c in route_copies + pos_copies(0):
        c.start()

    for c in inputs:
        c.wait()
    for t in range(steps):
        for i in range(cx):
            mod[t, i, 0:cy, :] = stiff_ref[:, i, :] * alive_ref[t, :, i, :].astype(F32)
    for c in range(4):
        for i in range(cx):
            mod[steps + c, i, 0:cy, :] = 0.125 * (load_ref[c, :, i, :] if c < 3 else dens_ref[:, i, :])
    rim = jnp.zeros((rows, cz), F32)
    for c in range(4):
        q = sum_x(mod[steps + c])
        q = q + roll(q, 1, 1)
        r = roll(q, 1, 2)
        load_f[c] = q + jnp.where(lane3 > 0, r, 0.0)
        for i in range(nx):
            at = c * nx + i
            rim = rim + jnp.where(lanes == at, roll(r[i], at, 1), 0.0)
    load_r[...] = rim

    ids = nodes_ref[...]
    row = lax.shift_right_logical(ids, jnp.full(ids.shape, cz.bit_length() - 1, jnp.int32))
    lane = ids & (cz - 1)
    grid_rows = cx * cy
    lane_t = jnp.transpose(jnp.concatenate([lane.astype(F32), jnp.zeros((128 - sb, 128), F32)], axis=0))
    for s in range(sb):
        row_pick[s] = (iota((grid_rows, 128), 0) == row[s:s + 1, :]).astype(F32).astype(BF16)
        hot = (iota((cz, 128), 0) == lane[s:s + 1, :]).astype(F32).astype(BF16)
        lane_pick[s, 0:cz, :] = hot
        lane_pick[s, cz:2 * cz, :] = hot
        col = jnp.broadcast_to(lane_t[:, s:s + 1], (128, cz))
        hot = (iota((128, cz), 1).astype(F32) == col).astype(F32).astype(BF16)
        lane_turn[s * 256:s * 256 + 128, :] = hot
        lane_turn[s * 256 + 128:s * 256 + 256, :] = hot

    def wait_all(copies):
        for c in copies:
            c.wait()

    wait_all(route_copies)
    upper = (iota((128, 128), 0) <= iota((128, 128), 1)).astype(F32)
    own = route_all[iz]
    for b in range(nz):
        hits = (route_all[b] == iz).astype(F32)
        rank_in[b] = jnp.where(hits > 0, jnp.dot(hits, upper, preferred_element_type=F32), 0.0)
    slot8 = nz * 8
    picks = []
    for b in range(nz):
        hits = (own == b).astype(F32)
        picks.append(jnp.where(hits > 0, jnp.dot(hits, upper, preferred_element_type=F32), 0.0))
    ranks8 = (iota((8, 128), 0) + 1).astype(F32)
    live8 = iota((8, 128), 0) < cap
    wide = 4 * npair
    spread4 = (lax.shift_right_logical(iota((npair, wide), 1), jnp.full((npair, wide), 2, jnp.int32))
               == iota((npair, wide), 0)).astype(F32)
    for t in range(steps):
        parts = [jnp.where((picks[b][t:t + 1, :] == ranks8) & live8, 1.0, 0.0) for b in range(nz)]
        table = jnp.concatenate(parts + [jnp.zeros((128 - slot8, 128), F32)], axis=0)
        back_pick[t] = jnp.transpose(table)[0:sb, :]
        hots = [jnp.where(rank_in[b, t:t + 1, :] == ranks8[0:cap], 1.0, 0.0) for b in range(nz)]
        table = jnp.concatenate([roll(hots[b], b * sb, 1) for b in range(nz)], axis=0)
        choose[t] = table
        live = jnp.sum(table, axis=1, keepdims=True)
        pair4 = bdot(pairt_ref[t].astype(F32), spread4)
        slot = iota((nslots, wide), 0).astype(F32)
        is_first = pair4[0:1, :] == slot
        both = (jnp.sum(jnp.where(is_first, live, 0.0), axis=0, keepdims=True)
                * jnp.sum(jnp.where(pair4[1:2, :] == slot, live, 0.0), axis=0, keepdims=True))
        hot = jnp.where(is_first, both, 0.0)
        part = iota((nslots, wide), 1) & 3
        for c in range(4):
            pair_hot[t, c * nslots:(c + 1) * nslots, :] = jnp.where(part == c, hot, 0.0).astype(BF16)

    ones = jnp.ones((nslots, 128), F32)

    def put(ref, at, value):
        ref[pl.ds(at, nslots, stride=FEATURES), :] = value

    for at in (3, 28, 29):
        put(feat_b, at, ones)
    for at in (19, 23, 27):
        put(feat_a, at, ones)

    def gather(phase):
        for c in range(3):
            for i in range(cx):
                flat[c * grid_rows + i * cy:c * grid_rows + (i + 1) * cy, :] = disp[c, i, 0:cy, :]
        high, low = split2(flat[...])
        left = jnp.concatenate([high, low], axis=1)
        for s in range(0, sb, 2):
            got = bdot(left, jnp.concatenate([lane_pick[s], lane_pick[s + 1]], axis=1))
            for h in range(2):
                mask = iota((grid_rows, 128), 0) == row[s + h:s + h + 1, :]
                for c in range(3):
                    part = jnp.where(mask, got[c * grid_rows:(c + 1) * grid_rows, h * 128:(h + 1) * 128], 0.0)
                    pos_all[phase, iz, s + h:s + h + 1, c * 128:(c + 1) * 128] = (
                        jnp.sum(part, axis=0, keepdims=True) + coords_ref[c, s + h:s + h + 1, :])

    def build_slots(t, phase):
        parts = split3(STRETCH * pos_all[phase].reshape(nz * sb, 384))
        got = bdot(choose[t, :, 0:nz * sb].astype(BF16), jnp.concatenate([p.astype(BF16) for p in parts], axis=1))
        norm = jnp.zeros((nslots, 128), F32)
        for c in range(3):
            high, middle, low = (got[:, k * 384 + c * 128:k * 384 + (c + 1) * 128] for k in range(3))
            x = high + middle + low
            slots[c] = x
            norm = norm - 0.5 * (x * x)
            for at in (0, 16, 20):
                put(feat_b, at + c, high)
            for at in (4, 24):
                put(feat_b, at + c, middle)
            put(feat_b, 8 + c, low)
            for at in (0, 8, 24):
                put(feat_a, at + c, high)
            for at in (4, 16):
                put(feat_a, at + c, middle)
            put(feat_a, 20 + c, low)
        for value, at_b, at_a in zip(split3(norm), (27, 23, 19), (3, 28, 29)):
            put(feat_b, at_b, value)
            put(feat_a, at_a, value)
        for k in range(nslots):
            at = k * FEATURES
            tile = feat_a[at:at + FEATURES, :].astype(BF16)
            take_a[k] = jnp.concatenate([tile] * 4, axis=0)
            give_b[k] = feat_b[at:at + 16, :].astype(BF16)
        for g in range(nslots // 4):
            turned = jnp.transpose(feat_b[g * 128:(g + 1) * 128, :])
            for k in range(4):
                mine = (iota((128, 128), 1) >= k * FEATURES) & (iota((128, 128), 1) < (k + 1) * FEATURES)
                turned_b[4 * g + k] = jnp.where(mine, turned, 0.0).astype(BF16)

    upper_half = iota((8, 128), 0) < 4

    def pair_range(t, start, stop):
        def one(q):
            p = pair_ref[t, 0, q]
            r = pair_ref[t, 1, q]
            w = jnp.exp2(bdot(turned_b[r], take_a[p]))
            high, low = split2(w)
            give = give_b[r]
            out = bdot(jnp.concatenate([give, give], axis=1), jnp.concatenate([high, low], axis=0))
            out = out[0:8] + out[8:16]
            return out + roll(out, 4, 0)

        def some(at, carry):
            for u in range(0, UNROLL, 2):
                q = start + at * UNROLL + u
                two = jnp.where(upper_half, one(q), one(q + 1))
                partial[pl.ds(pl.multiple_of(q * 4, 8), 8), :] = two
            return carry

        lax.fori_loop(0, (stop - start) // UNROLL, some, 0)

    def finish_pairs(t):
        total = jnp.zeros((4 * nslots, 128), F32)
        for piece in split3(partial[...]):
            total = total + bdot(pair_hot[t], piece.astype(BF16))
        weight = total[3 * nslots:4 * nslots]
        for c in range(3):
            force = (slots[c] * weight - total[c * nslots:(c + 1) * nslots]) * (REPULSION / STRETCH)
            for b in range(nz):
                send_f[t, b, 0:cap, c * 128:(c + 1) * 128] = force[b * cap:(b + 1) * cap]
        for c in ret_copies(t):
            c.start()
        ret[t, iz] = send_f[t, iz]

    def scatter(t):
        wait_all(ret_copies(t))
        halves = split2(ret[t].reshape(slot8, 384))
        force = bdot(back_pick[t, :, 0:slot8].astype(BF16), jnp.concatenate(halves, axis=1))
        for c in range(3):
            for s in range(sb):
                for h in range(2):
                    at = h * 384 + c * 128
                    line = jnp.broadcast_to(force[s:s + 1, at:at + 128], (16, 128)).astype(BF16)
                    spread = row_pick[s].reshape(grid_rows // 16, 16, 128) * line[None]
                    scatter_l[2 * s + h, c * grid_rows:(c + 1) * grid_rows, :] = spread.reshape(grid_rows, 128)
        left = jnp.concatenate([scatter_l[k] for k in range(2 * sb)], axis=1)
        touch[...] = bdot(left, lane_turn[...])

    def corners(field, rim_value, c):
        u = field[c]
        edge = jnp.stack([roll(rim_value, -(c * nx + i), 1) for i in range(nx)])
        above = roll(jnp.where(lane3 == 0, edge, u), -1, 2)
        both = u + above
        step = above - u
        shifted = roll(both, -1, 1)
        return both + shifted, shifted - both, step + roll(step, -1, 1)

    def stress_of(modulus):
        grads = []
        rim_value = disp_r[...]
        for c in range(3):
            mean, along_y, along_z = corners(disp, rim_value, c)
            grads.append((0.25 * (mean[1:] - mean[:-1]), 0.25 * (along_y[1:] + along_y[:-1]),
                          0.25 * (along_z[1:] + along_z[:-1])))
        trace = grads[0][0] + grads[1][1] + grads[2][2]
        return (modulus * (2.0 * grads[0][0] + trace), modulus * (2.0 * grads[1][1] + trace),
                modulus * (2.0 * grads[2][2] + trace), modulus * (grads[0][1] + grads[1][0]),
                modulus * (grads[1][2] + grads[2][1]), modulus * (grads[0][2] + grads[2][0]))

    def internal(t):
        s = stress_of(mod[t])
        table = ((s[0], s[3], s[5]), (s[3], s[1], s[4]), (s[5], s[4], s[2]))
        rim = load_r[...]
        for c in range(3):
            a0 = -0.25 * diff_x(table[c][0])
            ay = -0.25 * sum_x(table[c][1])
            az = -0.25 * sum_x(table[c][2])
            a = (a0 - ay) + roll(a0 + ay, 1, 1)
            b = az + roll(az, 1, 1)
            r = roll(a + b, 1, 2)
            big_f[c] = load_f[c] + (a - b) + jnp.where(lane3 > 0, r, 0.0)
            for i in range(nx):
                at = c * nx + i
                rim = rim + jnp.where(lanes == at, roll(r[i], at, 1), 0.0)
        rim_f[...] = rim

    line_lanes = iota((1, cz), 1)
    row_at = iota((rows, cz), 0)

    def halo_copies(t, comps, used):
        out = []
        for n, d in enumerate(ways):
            wx, wy, wz = (0 if step < 0 else 1 for step in d)
            dx, dy, dz = d
            if dz and dy:
                pair = line_send.at[t, wz, wy], line_recv.at[t, wz, wy, dx + 1]
            elif dz and dx:
                pair = z_send.at[t, wz], zx_recv.at[t, wz, wx]
            elif dz:
                pair = z_send.at[t, wz], z_recv.at[t, wz]
            elif dx and dy:
                pair = edge_send.at[t, wx, wy], edge_recv.at[t, wx, wy]
            elif dx:
                pair = x_send.at[t, wx, 0:comps + 1], x_recv.at[t, wx, 0:comps + 1]
            else:
                pair = y_send.at[t, wy, 0:used], y_recv.at[t, wy, 0:used]
            out.append(pltpu.make_async_remote_copy(
                src_ref=pair[0], dst_ref=pair[1], send_sem=halo_ss.at[t, n], recv_sem=halo_rs.at[t, n],
                device_id=neighbor(d), device_id_type=MESH))
        return out

    def halo(t, filler):
        comps = 4 if t == 0 else 3
        used = -(-(1 + comps * nx) // 8) * 8
        lines = ((0, 0), (1, cy))
        packed = jnp.zeros((rows, cz), F32)
        for c in range(comps):
            for i in range(nx):
                at = c * nx + i
                packed = jnp.where(lanes == at, roll(big_f[c, i], at, 1), packed)
        z_send[t, 0] = packed
        z_send[t, 1] = rim_f[...]
        for wy, line in lines:
            line_send[t, 0, wy] = packed[line:line + 1]
            line_send[t, 1, wy] = rim_f[line:line + 1]
        for wx, plane in ((0, 0), (1, cx)):
            x_send[t, wx, 0] = rim_f[...]
            for c in range(comps):
                x_send[t, wx, 1 + c] = big_f[c, plane]
            for wy, line in lines:
                edge_send[t, wx, wy, 0:1] = rim_f[line:line + 1]
                for c in range(comps):
                    edge_send[t, wx, wy, 1 + c:2 + c] = big_f[c, plane, line:line + 1]
        for wy, line in lines:
            y_send[t, wy, 0:1] = rim_f[line:line + 1]
            for c in range(comps):
                for i in range(nx):
                    at = 1 + c * nx + i
                    y_send[t, wy, at:at + 1] = big_f[c, i, line:line + 1]
        copies = halo_copies(t, comps, used)
        for copy, here in zip(copies, sends):
            @pl.when(here)
            def _():
                copy.start()

        filler()
        for copy, here, back in zip(copies, sends, gets):
            @pl.when(here)
            def _():
                copy.wait_send()

            @pl.when(back)
            def _():
                copy.wait_recv()

        def across(tile, wx):
            at = line_lanes if tile.shape[0] == 1 else lanes
            mine = functools.reduce(jnp.logical_or, [at == c * nx + (0 if wx else cx) for c in range(comps)])
            return jnp.where(mine, roll(tile, -cx if wx else cx, 1), 0.0)

        def fold(base, faces, edges, corners_):
            for wx in range(2):
                base = base + across(faces[wx], wx)
            for wy, line in ((1, 0), (0, cy)):
                value = edges[wy] + across(corners_[0][wy], 0) + across(corners_[1][wy], 1)
                base = base + jnp.where(row_at == line, value, 0.0)
            return base

        folded = [fold(z_recv[t, w], [zx_recv[t, w, wx] for wx in range(2)], [line_recv[t, w, wy, 1] for wy in range(2)],
                       [[line_recv[t, w, wy, 2 * wx] for wy in range(2)] for wx in range(2)]) for w in range(2)]
        rim_f[...] = folded[0] + fold(
            rim_f[...], [x_recv[t, wx, 0] for wx in range(2)], [y_recv[t, wy, 0:1] for wy in range(2)],
            [[edge_recv[t, wx, wy, 0:1] for wy in range(2)] for wx in range(2)])
        for c in range(comps):
            big_f[c, 0] = big_f[c, 0] + x_recv[t, 1, 1 + c]
            big_f[c, cx] = big_f[c, cx] + x_recv[t, 0, 1 + c]
        for wy, line in ((1, 0), (0, cy)):
            for c in range(comps):
                for i in range(nx):
                    at = 1 + c * nx + i
                    add = y_recv[t, wy, at:at + 1]
                    if i in (0, cx):
                        wx = 1 if i == 0 else 0
                        add = add + edge_recv[t, wx, wy, 1 + c:2 + c]
                    big_f[c, i, line:line + 1] = big_f[c, i, line:line + 1] + add
        for c in range(comps):
            for i in range(nx):
                at = c * nx + i
                big_f[c, i] = big_f[c, i] + jnp.where(lanes == 0, roll(folded[1], -at, 1), 0.0)

    early = npair // 4 // UNROLL * UNROLL

    def contact(t, phase):
        if phase > 0:
            wait_all(pos_copies(phase))
            build_slots(t, phase)
            pair_range(t, 0, npair)
        else:
            pair_range(t, early, npair)
        finish_pairs(t)

    wait_all(pos_copies(0))
    build_slots(0, 0)
    pair_range(0, 0, npair)
    finish_pairs(0)
    build_slots(1, 0)
    pair_range(1, 0, early)

    for t in range(steps):
        if t == 0:
            big_f[...] = load_f[...]
            rim_f[...] = load_r[...]
        else:
            if t + 1 < steps:
                gather(t)
                for c in pos_copies(t):
                    c.start()
            internal(t)
        scatter(t)
        for c in range(3):
            for i in range(cx):
                at = c * grid_rows + i * cy
                big_f[c, i, 0:cy, :] = big_f[c, i, 0:cy, :] + touch[at:at + cy, :]
        halo(t, functools.partial(contact, t + 1, t) if t + 1 < steps else lambda: None)
        if t == 0:
            mass = big_f[3]
            minv[...] = jnp.where(mass > 0.0, 1.0 / mass, 0.0)
            held = jnp.where((lanes >= 3 * nx) & (lanes < 4 * nx), rim_f[...], 0.0)
            spread = roll(held, -3 * nx, 1) + roll(held, -2 * nx, 1) + roll(held, -nx, 1)
            minv_r[...] = jnp.where(spread > 0.0, 1.0 / spread, 0.0)
            for c in range(3):
                vel[c] = TIME_STEP * (big_f[c] * minv[...])
            vel_r[...] = TIME_STEP * (rim_f[...] * minv_r[...])
            disp[...] = TIME_STEP * vel[...]
            disp_r[...] = TIME_STEP * vel_r[...]
        else:
            for c in range(3):
                vel[c] = vel[c] + TIME_STEP * (big_f[c] * minv[...])
            vel_r[...] = vel_r[...] + TIME_STEP * (rim_f[...] * minv_r[...])
            disp[...] = disp[...] + TIME_STEP * vel[...]
            disp_r[...] = disp_r[...] + TIME_STEP * vel_r[...]

    rim_value = vel_r[...]
    for c in range(3):
        mean, _, _ = corners(vel, rim_value, c)
        mean = 0.125 * (mean[1:] + mean[:-1])
        for i in range(cx):
            vout_ref[c, :, i, :] = mean[i, 0:cy, :]
    s = stress_of(mod[steps - 1])
    for c in range(6):
        for i in range(cx):
            sout_ref[c, :, i, :] = s[c][i, 0:cy, :]


def per_device(stiffness, density, load, alive, surf_coords, surf_nodes, routes, pairs):
    cx, cy, cz = stiffness.shape
    steps = alive.shape[0]
    sb = surf_coords.shape[0]
    npair = pairs.shape[2]
    count_x, count_y, nz = (lax.axis_size(a) for a in ("gx", "gy", "gz"))
    cap = max(sb // 4, sb // nz)
    nx = cx + 1
    pairt = jnp.transpose(pairs[:, 0], (0, 2, 1))
    sizes = (count_x, count_y, cx, cy, cz, sb, npair, steps, nz, cap)
    nslots = nz * cap
    vm = lambda *shape: pltpu.VMEM(shape, F32)
    vh = lambda *shape: pltpu.VMEM(shape, BF16)
    dma = lambda *shape: pltpu.SemaphoreType.DMA(shape)
    column = max(nz - 1, 1)
    scratch = [
        vm(cy, cx, cz), vm(cy, cx, cz), vm(3, cy, cx, cz), pltpu.VMEM((steps, cy, cx, cz), jnp.int32), dma(4),
        vm(steps + 4, cx, 16, cz), vm(4, nx, 16, cz), vm(16, cz), vm(4, nx, 16, cz), vm(16, cz),
        vm(3, nx, 16, cz), vm(16, cz), vm(3, nx, 16, cz), vm(16, cz), vm(nx, 16, cz), vm(16, cz),
        pltpu.VMEM((nz, 8, 128), jnp.int32), vm(steps - 1, nz, sb, 384), vm(3, nslots, 128),
        vm(nslots * FEATURES, 128), vm(nslots * FEATURES, 128), vh(nslots, 128, 128), vh(nslots, 128, 128), vh(nslots, 16, 128),
        vm(4 * npair, 128), vm(steps, nz, 8, 384), vm(steps, nz, 8, 384), vm(steps, sb, 128), vm(steps, nslots, 128), vh(steps, 4 * nslots, 4 * npair), vm(nz, 8, 128),
        vh(sb, cx * cy, 128), vh(sb, 2 * cz, 128), vh(2 * sb * 128, cz), vm(3 * cx * cy, cz), vm(3 * cx * cy, cz),
        vh(2 * sb, 3 * cx * cy, 128),
        vm(steps, 2, 5, 16, cz), vm(steps, 2, 5, 16, cz), vm(steps, 2, 40, cz), vm(steps, 2, 40, cz),
        vm(steps, 2, 2, 8, cz), vm(steps, 2, 2, 8, cz),
        vm(steps, 2, 16, cz), vm(steps, 2, 16, cz), vm(steps, 2, 2, 16, cz), vm(steps, 2, 2, 1, cz), vm(steps, 2, 2, 3, 1, cz),
        dma(column), dma(column), dma(steps - 1, column), dma(steps - 1, column), dma(steps, column), dma(steps, column),
        dma(steps, 26), dma(steps, 26),
    ]
    vmem = pl.BlockSpec(memory_space=pltpu.VMEM)
    vel, stress = pl.pallas_call(
        functools.partial(body, sizes),
        out_shape=(jax.ShapeDtypeStruct((3, cy, cx, cz), F32), jax.ShapeDtypeStruct((6, cy, cx, cz), F32)),
        in_specs=[pl.BlockSpec(memory_space=pltpu.MemorySpace.HBM)] * 4 + [vmem] * 4 + [pl.BlockSpec(memory_space=pltpu.SMEM)],
        out_specs=(vmem, vmem),
        scratch_shapes=scratch,
        compiler_params=pltpu.CompilerParams(collective_id=0, has_side_effects=True, vmem_limit_bytes=56 * 1024 * 1024),
    )(jnp.swapaxes(stiffness, 0, 1), jnp.swapaxes(density, 0, 1), jnp.swapaxes(load, 1, 2), jnp.swapaxes(alive, 1, 2),
      jnp.swapaxes(surf_coords, 0, 1), surf_nodes, routes, pairt, pairt)
    return jnp.swapaxes(vel, 1, 2), jnp.swapaxes(stress, 1, 2)


def solution(mesh):
    return jax.shard_map(
        per_device,
        mesh=mesh,
        in_specs=(
            P("gx", "gy", "gz"),
            P("gx", "gy", "gz"),
            P(None, "gx", "gy", "gz"),
            P(None, "gx", "gy", "gz"),
            P(("gx", "gy", "gz"), None, None),
            P(("gx", "gy", "gz"), None),
            P(None, ("gx", "gy", "gz")),
            P(None, ("gx", "gy", "gz"), None, None),
        ),
        out_specs=(P(None, "gx", "gy", "gz"), P(None, "gx", "gy", "gz")),
        check_vma=False,
    )
```

time: 62.4 us -> 46.2 us (0.74)
  Pallas kernels: 59.1 us -> 42.9 us
    pallas_call x1, Pallas kernels: 59.1 us -> 42.9 us  [per_device(): pl.pallas_call(functools.partial(body, sizes), out_shape=(jax.ShapeDtypeS...]
where the time goes in v1:
time: 46.2 us; the launch traced here: 45.9 us
  Pallas kernels  42.9 us (93%)
  local copies, waits for them, and re-layouts  2.34 us (5%)
  between operations  0.65 us (1%)
    pallas_call x1, Pallas kernels, per_device(): pl.pallas_call(functools.partial(body, sizes), out_shape=(jax.ShapeDtypeS...  42.9 us
    unnamed x4, local copies, waits for them, and re-layouts  2.34 us

profile of v1, /device:TPU:1, one launch (start us, length us, event | category | flops | bytes accessed | tf_op | source)
XLA Modules:
  0.0 45.9 jit_solution(11636859083645104260)
XLA Ops:
  0.6 42.9 %shard_map.95 = (f32[3,12,8,128]{3,2,1,0:T(8,128)}, f32[6,12,8,128]{3,2,1,0:T(8,128)}) custom-call(f32[12,8,128]{2,1,0:T(8,128)} %bitcast.14, f32[12,8,128]{2,1,0:T(8,128)} %bitcast.15, f32[3,12,8,128]{3,2,1,0:T(8,128)} %bitcast.13, s32[4,12,8,128]{3,2,1,0:T(8,128)} %bitcast.11, f32[3,16,128]{2,1,0:T(8,128)} %bitcast.16, s32[16,128]{1,0:T(8,128)} %nodes_ref.1, ...), custom_call_target="tpu_custom_call" | custom-call | tf_op jit(solution)/shard_map/pallas_call | solution.py:550
  43.6 0.0 copy-start
  43.6 1.6 %copy.12 = f32[3,8,12,128]{3,1,2,0:T(8,128)} copy(f32[3,8,12,128]{3,1,2,0:T(8,128)} %bitcast.12) | data formatting | bytes 294912
  45.2 0.0 copy-done
  45.2 0.7 %copy.13 = f32[6,8,12,128]{3,1,2,0:T(8,128)} copy(f32[6,8,12,128]{3,1,2,0:T(8,128)S(1)} %bitcast.10) | data formatting | bytes 589824
Async XLA Ops:
  43.6 1.6 %copy-start = (f32[6,12,8,128]{3,2,1,0:T(8,128)S(1)}, f32[6,12,8,128]{3,2,1,0:T(8,128)}, u32[]{:S(2)}) copy-start(f32[6,12,8,128]{3,2,1,0:T(8,128)} %get-tuple-element.5) | copy-start | bytes 884740

commit v2 on v1

--- a/solution.py
+++ b/solution.py
@@ -18,7 +18,7 @@
 BF16 = jnp.bfloat16
 STRETCH = math.sqrt(2.0 * math.log2(math.e) / KERNEL_SCALE)
 FEATURES = 32
-UNROLL = 16
+UNROLL = 32
 
 
 def iota(shape, dim):
@@ -55,7 +55,7 @@
 
 def body(sizes, stiff_hbm, dens_hbm, load_hbm, alive_hbm, coords_ref, nodes_ref, routes_ref, pairt_ref, pair_ref,
          vout_ref, sout_ref, *scratch):
-    (stiff_ref, dens_ref, load_ref, alive_ref, in_sem, mod, big_f, rim_f, load_f, load_r, vel, vel_r, disp, disp_r, minv, minv_r, route_all, pos_all, slots, feat_a, feat_b, take_a, turned_b, give_b,
+    (stiff_ref, dens_ref, load_ref, alive_ref, in_sem, mod, big_f, rim_f, load_f, load_r, vel, vel_r, disp, disp_r, minv, minv_r, route_all, pos_all, slots, parts, take_a, turned_b, give_b,
      partial, send_f, ret, back_pick, choose, pair_hot, rank_in, row_pick, lane_pick, lane_turn, flat, touch, scatter_l,
      x_send, x_recv, y_send, y_recv, edge_send, edge_recv, z_send, z_recv, zx_recv, line_send, line_recv,
      route_ss, route_rs, pos_ss, pos_rs, ret_ss, ret_rs, halo_ss, halo_rs) = scratch
@@ -75,18 +75,23 @@
     for c in inputs:
         c.start()
 
-    for ref in (x_recv, y_send, y_recv, edge_recv, z_recv, zx_recv, line_recv, mod, feat_a, feat_b, send_f):
-        ref[...] = jnp.zeros(ref.shape, ref.dtype)
+    def clear(*refs):
+        for ref in refs:
+            ref[...] = jnp.zeros(ref.shape, ref.dtype)
+
+    clear(x_recv, y_recv, edge_recv, z_recv, zx_recv, line_recv)
 
     sides = (("gx", ix, count_x), ("gy", iy, count_y), ("gz", iz, nz))
-    ways = sorted((d for d in itertools.product((-1, 0, 1), repeat=3) if any(d)), key=lambda d: (-abs(d[2]), -sum(map(abs, d))))
+    only_z = nz == 2
+    ways = sorted((d for d in itertools.product((-1, 0, 1), repeat=3) if any(d) and not (only_z and d[2] < 0)), key=lambda d: (-abs(d[2]), -sum(map(abs, d))))
 
     def there(d, sign):
         return functools.reduce(jnp.logical_and, [
-            (at + sign * step >= 0) & (at + sign * step < count) for step, (_, at, count) in zip(d, sides) if step])
+            (at + sign * step >= 0) & (at + sign * step < count)
+            for step, (name, at, count) in zip(d, sides) if step and not (only_z and name == "gz")] or [jnp.bool_(True)])
 
     def neighbor(d):
-        return {name: at + step for step, (name, at, _) in zip(d, sides) if step}
+        return {name: 1 - at if only_z and name == "gz" else at + step for step, (name, at, _) in zip(d, sides) if step}
 
     sends = [there(d, 1) for d in ways]
     gets = [there(d, -1) for d in ways]
@@ -131,6 +136,7 @@
     for c in route_copies + pos_copies(0):
         c.start()
 
+    clear(mod, parts, send_f, y_send)
     for c in inputs:
         c.wait()
     for t in range(steps):
@@ -154,16 +160,17 @@
     row = lax.shift_right_logical(ids, jnp.full(ids.shape, cz.bit_length() - 1, jnp.int32))
     lane = ids & (cz - 1)
     grid_rows = cx * cy
-    lane_t = jnp.transpose(jnp.concatenate([lane.astype(F32), jnp.zeros((128 - sb, 128), F32)], axis=0))
+    half_rows = grid_rows // 2
+    row2 = lax.shift_right_logical(row, jnp.ones(row.shape, jnp.int32))
+    lane2 = lane + (row & 1) * cz
+    lane_t = jnp.transpose(jnp.concatenate([lane2.astype(F32), jnp.zeros((128 - sb, 128), F32)], axis=0))
     for s in range(sb):
-        row_pick[s] = (iota((grid_rows, 128), 0) == row[s:s + 1, :]).astype(F32).astype(BF16)
+        row_pick[s] = (iota((half_rows, 128), 0) == row2[s:s + 1, :]).astype(F32).astype(BF16)
         hot = (iota((cz, 128), 0) == lane[s:s + 1, :]).astype(F32).astype(BF16)
         lane_pick[s, 0:cz, :] = hot
         lane_pick[s, cz:2 * cz, :] = hot
-        col = jnp.broadcast_to(lane_t[:, s:s + 1], (128, cz))
-        hot = (iota((128, cz), 1).astype(F32) == col).astype(F32).astype(BF16)
-        lane_turn[s * 256:s * 256 + 128, :] = hot
-        lane_turn[s * 256 + 128:s * 256 + 256, :] = hot
+        col = jnp.broadcast_to(lane_t[:, s:s + 1], (128, 2 * cz))
+        lane_turn[s * 128:(s + 1) * 128, :] = (iota((128, 2 * cz), 1).astype(F32) == col).astype(F32).astype(BF16)
 
     def wait_all(copies):
         for c in copies:
@@ -186,8 +193,8 @@
     spread4 = (lax.shift_right_logical(iota((npair, wide), 1), jnp.full((npair, wide), 2, jnp.int32))
                == iota((npair, wide), 0)).astype(F32)
     for t in range(steps):
-        parts = [jnp.where((picks[b][t:t + 1, :] == ranks8) & live8, 1.0, 0.0) for b in range(nz)]
-        table = jnp.concatenate(parts + [jnp.zeros((128 - slot8, 128), F32)], axis=0)
+        rows_ = [jnp.where((picks[b][t:t + 1, :] == ranks8) & live8, 1.0, 0.0) for b in range(nz)]
+        table = jnp.concatenate(rows_ + [jnp.zeros((128 - slot8, 128), F32)], axis=0)
         back_pick[t] = jnp.transpose(table)[0:sb, :]
         hots = [jnp.where(rank_in[b, t:t + 1, :] == ranks8[0:cap], 1.0, 0.0) for b in range(nz)]
         table = jnp.concatenate([roll(hots[b], b * sb, 1) for b in range(nz)], axis=0)
@@ -203,15 +210,13 @@
         for c in range(4):
             pair_hot[t, c * nslots:(c + 1) * nslots, :] = jnp.where(part == c, hot, 0.0).astype(BF16)
 
-    ones = jnp.ones((nslots, 128), F32)
-
-    def put(ref, at, value):
-        ref[pl.ds(at, nslots, stride=FEATURES), :] = value
-
-    for at in (3, 28, 29):
-        put(feat_b, at, ones)
-    for at in (19, 23, 27):
-        put(feat_a, at, ones)
+    at8 = iota((8, 128), 0)
+    upper_half = at8 < 4
+    last = (at8 & 3) == 3
+    blank = jnp.zeros((8, 128), F32)
+
+    def put(at, value):
+        parts[pl.ds(at, nslots, stride=16), :] = value
 
     def gather(phase):
         for c in range(3):
@@ -229,56 +234,53 @@
                         jnp.sum(part, axis=0, keepdims=True) + coords_ref[c, s + h:s + h + 1, :])
 
     def build_slots(t, phase):
-        parts = split3(STRETCH * pos_all[phase].reshape(nz * sb, 384))
-        got = bdot(choose[t, :, 0:nz * sb].astype(BF16), jnp.concatenate([p.astype(BF16) for p in parts], axis=1))
+        pieces = split3(STRETCH * pos_all[phase].reshape(nz * sb, 384))
+        got = bdot(choose[t, :, 0:nz * sb].astype(BF16), jnp.concatenate([p.astype(BF16) for p in pieces], axis=1))
         norm = jnp.zeros((nslots, 128), F32)
         for c in range(3):
             high, middle, low = (got[:, k * 384 + c * 128:k * 384 + (c + 1) * 128] for k in range(3))
             x = high + middle + low
             slots[c] = x
             norm = norm - 0.5 * (x * x)
-            for at in (0, 16, 20):
-                put(feat_b, at + c, high)
-            for at in (4, 24):
-                put(feat_b, at + c, middle)
-            put(feat_b, 8 + c, low)
-            for at in (0, 8, 24):
-                put(feat_a, at + c, high)
-            for at in (4, 16):
-                put(feat_a, at + c, middle)
-            put(feat_a, 20 + c, low)
-        for value, at_b, at_a in zip(split3(norm), (27, 23, 19), (3, 28, 29)):
-            put(feat_b, at_b, value)
-            put(feat_a, at_a, value)
+            for k, value in enumerate((high, middle, low)):
+                put(4 * k + c, value)
+        for k, value in enumerate(split3(norm)):
+            put(4 * k + 3, value)
         for k in range(nslots):
-            at = k * FEATURES
-            tile = feat_a[at:at + FEATURES, :].astype(BF16)
-            take_a[k] = jnp.concatenate([tile] * 4, axis=0)
-            give_b[k] = feat_b[at:at + 16, :].astype(BF16)
-        for g in range(nslots // 4):
-            turned = jnp.transpose(feat_b[g * 128:(g + 1) * 128, :])
-            for k in range(4):
-                mine = (iota((128, 128), 1) >= k * FEATURES) & (iota((128, 128), 1) < (k + 1) * FEATURES)
-                turned_b[4 * g + k] = jnp.where(mine, turned, 0.0).astype(BF16)
-
-    upper_half = iota((8, 128), 0) < 4
+            main = parts[k * 16:k * 16 + 8, :]
+            rest = parts[k * 16 + 8:k * 16 + 16, :]
+            swapped = roll(main, 4, 0)
+            ones_b = jnp.where(last, 1.0, main)
+            tile_b = [main, jnp.where(upper_half, rest, jnp.where(at8 == 7, 1.0, swapped)), ones_b, blank]
+            tile_a = [jnp.where(last, 1.0, jnp.where(upper_half, main, swapped)), jnp.where(at8 == 3, 1.0, main),
+                      jnp.where(upper_half, rest, jnp.where(at8 == 7, swapped, main)), blank]
+            give = [jnp.where(at8 == 7, 0.0, ones_b), jnp.where(at8 < 3, rest, 0.0)]
+            take_a[k] = jnp.concatenate(tile_a, axis=0).astype(BF16)
+            give_b[k] = jnp.concatenate(give, axis=0).astype(BF16)
+            turned_b[k] = jnp.transpose(jnp.concatenate(tile_b, axis=0)).astype(BF16)
+
 
     def pair_range(t, start, stop):
-        def one(q):
+        def weigh(q):
             p = pair_ref[t, 0, q]
             r = pair_ref[t, 1, q]
-            w = jnp.exp2(bdot(turned_b[r], take_a[p]))
-            high, low = split2(w)
-            give = give_b[r]
+            return bdot(turned_b[r], take_a[p]), give_b[r]
+
+        def gain(exponent, give):
+            high, low = split2(jnp.exp2(exponent))
             out = bdot(jnp.concatenate([give, give], axis=1), jnp.concatenate([high, low], axis=0))
             out = out[0:8] + out[8:16]
             return out + roll(out, 4, 0)
 
         def some(at, carry):
+            first = start + at * UNROLL
+            ahead = weigh(first)
             for u in range(0, UNROLL, 2):
-                q = start + at * UNROLL + u
-                two = jnp.where(upper_half, one(q), one(q + 1))
-                partial[pl.ds(pl.multiple_of(q * 4, 8), 8), :] = two
+                both = []
+                for k in (u, u + 1):
+                    now, ahead = ahead, weigh(first + k + 1) if k + 1 < UNROLL else None
+                    both.append(gain(*now))
+                partial[pl.ds(pl.multiple_of((first + u) * 4, 8), 8), :] = jnp.where(upper_half, *both)
             return carry
 
         lax.fori_loop(0, (stop - start) // UNROLL, some, 0)
@@ -297,18 +299,21 @@
         ret[t, iz] = send_f[t, iz]
 
     def scatter(t):
-        wait_all(ret_copies(t))
         halves = split2(ret[t].reshape(slot8, 384))
         force = bdot(back_pick[t, :, 0:slot8].astype(BF16), jnp.concatenate(halves, axis=1))
-        for c in range(3):
-            for s in range(sb):
-                for h in range(2):
+        for s in range(sb):
+            for h in range(2):
+                for c in range(3):
                     at = h * 384 + c * 128
                     line = jnp.broadcast_to(force[s:s + 1, at:at + 128], (16, 128)).astype(BF16)
-                    spread = row_pick[s].reshape(grid_rows // 16, 16, 128) * line[None]
-                    scatter_l[2 * s + h, c * grid_rows:(c + 1) * grid_rows, :] = spread.reshape(grid_rows, 128)
-        left = jnp.concatenate([scatter_l[k] for k in range(2 * sb)], axis=1)
-        touch[...] = bdot(left, lane_turn[...])
+                    spread = row_pick[s].reshape(half_rows // 16, 16, 128) * line[None]
+                    at = (3 * h + c) * half_rows
+                    scatter_l[s, at:at + half_rows, :] = spread.reshape(half_rows, 128)
+        left = jnp.concatenate([scatter_l[s] for s in range(sb)], axis=1)
+        total = bdot(left, lane_turn[...])
+        total = total[0:3 * half_rows] + total[3 * half_rows:]
+        for odd in range(2):
+            touch[pl.ds(odd, 3 * half_rows, stride=2), :] = total[:, odd * cz:(odd + 1) * cz]
 
     def corners(field, rim_value, c):
         u = field[c]
@@ -356,6 +361,8 @@
         for n, d in enumerate(ways):
             wx, wy, wz = (0 if step < 0 else 1 for step in d)
             dx, dy, dz = d
+            if only_z:
+                wz = 1 - iz
             if dz and dy:
                 pair = line_send.at[t, wz, wy], line_recv.at[t, wz, wy, dx + 1]
             elif dz and dx:
@@ -452,7 +459,7 @@
                 at = c * nx + i
                 big_f[c, i] = big_f[c, i] + jnp.where(lanes == 0, roll(folded[1], -at, 1), 0.0)
 
-    early = npair // 4 // UNROLL * UNROLL
+    early = npair // 2 // UNROLL * UNROLL
 
     def contact(t, phase):
         if phase > 0:
@@ -474,11 +481,13 @@
         if t == 0:
             big_f[...] = load_f[...]
             rim_f[...] = load_r[...]
+            wait_all(ret_copies(t))
         else:
             if t + 1 < steps:
                 gather(t)
                 for c in pos_copies(t):
                     c.start()
+            wait_all(ret_copies(t))
             internal(t)
         scatter(t)
         for c in range(3):
@@ -536,10 +545,10 @@
         vm(steps + 4, cx, 16, cz), vm(4, nx, 16, cz), vm(16, cz), vm(4, nx, 16, cz), vm(16, cz),
         vm(3, nx, 16, cz), vm(16, cz), vm(3, nx, 16, cz), vm(16, cz), vm(nx, 16, cz), vm(16, cz),
         pltpu.VMEM((nz, 8, 128), jnp.int32), vm(steps - 1, nz, sb, 384), vm(3, nslots, 128),
-        vm(nslots * FEATURES, 128), vm(nslots * FEATURES, 128), vh(nslots, 128, 128), vh(nslots, 128, 128), vh(nslots, 16, 128),
+        vm(nslots * 16, 128), vh(nslots, FEATURES, 128), vh(nslots, 128, FEATURES), vh(nslots, 16, 128),
         vm(4 * npair, 128), vm(steps, nz, 8, 384), vm(steps, nz, 8, 384), vm(steps, sb, 128), vm(steps, nslots, 128), vh(steps, 4 * nslots, 4 * npair), vm(nz, 8, 128),
-        vh(sb, cx * cy, 128), vh(sb, 2 * cz, 128), vh(2 * sb * 128, cz), vm(3 * cx * cy, cz), vm(3 * cx * cy, cz),
-        vh(2 * sb, 3 * cx * cy, 128),
+        vh(sb, cx * cy // 2, 128), vh(sb, 2 * cz, 128), vh(sb * 128, 2 * cz), vm(3 * cx * cy, cz), vm(3 * cx * cy, cz),
+        vh(sb, 3 * cx * cy, 128),
         vm(steps, 2, 5, 16, cz), vm(steps, 2, 5, 16, cz), vm(steps, 2, 40, cz), vm(steps, 2, 40, cz),
         vm(steps, 2, 2, 8, cz), vm(steps, 2, 2, 8, cz),
         vm(steps, 2, 16, cz), vm(steps, 2, 16, cz), vm(steps, 2, 2, 16, cz), vm(steps, 2, 2, 1, cz), vm(steps, 2, 2, 3, 1, cz),

time: 46.2 us -> 44 us (0.952)
  Pallas kernels: 42.9 us -> 40.8 us
    pallas_call x1, Pallas kernels: 42.9 us -> 40.8 us  [per_device(): pl.pallas_call(functools.partial(body, sizes), out_shape=(jax.ShapeDtypeS...]
where the time goes in v2:
time: 44 us; the launch traced here: 43.8 us
  Pallas kernels  40.8 us (93%)
  local copies, waits for them, and re-layouts  2.34 us (5%)
  between operations  0.65 us (1%)
    pallas_call x1, Pallas kernels, per_device(): pl.pallas_call(functools.partial(body, sizes), out_shape=(jax.ShapeDtypeS...  40.8 us
    unnamed x4, local copies, waits for them, and re-layouts  2.34 us

profile of v2, /device:TPU:1, one launch (start us, length us, event | category | flops | bytes accessed | tf_op | source)
XLA Modules:
  0.0 43.8 jit_solution(8919285488258502922)
XLA Ops:
  0.6 40.8 %shard_map.95 = (f32[3,12,8,128]{3,2,1,0:T(8,128)}, f32[6,12,8,128]{3,2,1,0:T(8,128)}) custom-call(f32[12,8,128]{2,1,0:T(8,128)} %bitcast.14, f32[12,8,128]{2,1,0:T(8,128)} %bitcast.15, f32[3,12,8,128]{3,2,1,0:T(8,128)} %bitcast.13, s32[4,12,8,128]{3,2,1,0:T(8,128)} %bitcast.11, f32[3,16,128]{2,1,0:T(8,128)} %bitcast.16, s32[16,128]{1,0:T(8,128)} %nodes_ref.1, ...), custom_call_target="tpu_custom_call" | custom-call | tf_op jit(solution)/shard_map/pallas_call | solution.py:559
  41.4 0.0 copy-start
  41.4 1.6 %copy.12 = f32[3,8,12,128]{3,1,2,0:T(8,128)} copy(f32[3,8,12,128]{3,1,2,0:T(8,128)} %bitcast.12) | data formatting | bytes 294912
  43.1 0.0 copy-done
  43.1 0.7 %copy.13 = f32[6,8,12,128]{3,1,2,0:T(8,128)} copy(f32[6,8,12,128]{3,1,2,0:T(8,128)S(1)} %bitcast.10) | data formatting | bytes 589824
Async XLA Ops:
  41.4 1.6 %copy-start = (f32[6,12,8,128]{3,2,1,0:T(8,128)S(1)}, f32[6,12,8,128]{3,2,1,0:T(8,128)}, u32[]{:S(2)}) copy-start(f32[6,12,8,128]{3,2,1,0:T(8,128)} %get-tuple-element.5) | copy-start | bytes 884740

commit v3 on v2

--- a/solution.py
+++ b/solution.py
@@ -18,7 +18,6 @@
 BF16 = jnp.bfloat16
 STRETCH = math.sqrt(2.0 * math.log2(math.e) / KERNEL_SCALE)
 FEATURES = 32
-UNROLL = 32
 
 
 def iota(shape, dim):
@@ -261,6 +260,8 @@
 
 
     def pair_range(t, start, stop):
+        count = stop - start
+
         def weigh(q):
             p = pair_ref[t, 0, q]
             r = pair_ref[t, 1, q]
@@ -273,17 +274,17 @@
             return out + roll(out, 4, 0)
 
         def some(at, carry):
-            first = start + at * UNROLL
+            first = start + at * count
             ahead = weigh(first)
-            for u in range(0, UNROLL, 2):
+            for u in range(0, count, 2):
                 both = []
                 for k in (u, u + 1):
-                    now, ahead = ahead, weigh(first + k + 1) if k + 1 < UNROLL else None
+                    now, ahead = ahead, weigh(first + k + 1) if k + 1 < count else None
                     both.append(gain(*now))
                 partial[pl.ds(pl.multiple_of((first + u) * 4, 8), 8), :] = jnp.where(upper_half, *both)
             return carry
 
-        lax.fori_loop(0, (stop - start) // UNROLL, some, 0)
+        lax.fori_loop(0, 1 + jnp.minimum(iz, 0), some, 0)
 
     def finish_pairs(t):
         total = jnp.zeros((4 * nslots, 128), F32)
@@ -329,21 +330,20 @@
         rim_value = disp_r[...]
         for c in range(3):
             mean, along_y, along_z = corners(disp, rim_value, c)
-            grads.append((0.25 * (mean[1:] - mean[:-1]), 0.25 * (along_y[1:] + along_y[:-1]),
-                          0.25 * (along_z[1:] + along_z[:-1])))
+            grads.append((mean[1:] - mean[:-1], along_y[1:] + along_y[:-1], along_z[1:] + along_z[:-1]))
         trace = grads[0][0] + grads[1][1] + grads[2][2]
         return (modulus * (2.0 * grads[0][0] + trace), modulus * (2.0 * grads[1][1] + trace),
                 modulus * (2.0 * grads[2][2] + trace), modulus * (grads[0][1] + grads[1][0]),
                 modulus * (grads[1][2] + grads[2][1]), modulus * (grads[0][2] + grads[2][0]))
 
     def internal(t):
-        s = stress_of(mod[t])
+        s = stress_of(-0.0625 * mod[t])
         table = ((s[0], s[3], s[5]), (s[3], s[1], s[4]), (s[5], s[4], s[2]))
         rim = load_r[...]
         for c in range(3):
-            a0 = -0.25 * diff_x(table[c][0])
-            ay = -0.25 * sum_x(table[c][1])
-            az = -0.25 * sum_x(table[c][2])
+            a0 = diff_x(table[c][0])
+            ay = sum_x(table[c][1])
+            az = sum_x(table[c][2])
             a = (a0 - ay) + roll(a0 + ay, 1, 1)
             b = az + roll(az, 1, 1)
             r = roll(a + b, 1, 2)
@@ -459,15 +459,11 @@
                 at = c * nx + i
                 big_f[c, i] = big_f[c, i] + jnp.where(lanes == 0, roll(folded[1], -at, 1), 0.0)
 
-    early = npair // 2 // UNROLL * UNROLL
-
     def contact(t, phase):
         if phase > 0:
             wait_all(pos_copies(phase))
             build_slots(t, phase)
             pair_range(t, 0, npair)
-        else:
-            pair_range(t, early, npair)
         finish_pairs(t)
 
     wait_all(pos_copies(0))
@@ -475,7 +471,7 @@
     pair_range(0, 0, npair)
     finish_pairs(0)
     build_slots(1, 0)
-    pair_range(1, 0, early)
+    pair_range(1, 0, npair)
 
     for t in range(steps):
         if t == 0:
@@ -519,7 +515,7 @@
         mean = 0.125 * (mean[1:] + mean[:-1])
         for i in range(cx):
             vout_ref[c, :, i, :] = mean[i, 0:cy, :]
-    s = stress_of(mod[steps - 1])
+    s = stress_of(0.25 * mod[steps - 1])
     for c in range(6):
         for i in range(cx):
             sout_ref[c, :, i, :] = s[c][i, 0:cy, :]
@@ -558,7 +554,7 @@
     vmem = pl.BlockSpec(memory_space=pltpu.VMEM)
     vel, stress = pl.pallas_call(
         functools.partial(body, sizes),
-        out_shape=(jax.ShapeDtypeStruct((3, cy, cx, cz), F32), jax.ShapeDtypeStruct((6, cy, cx, cz), F32)),
+        out_shape=(pltpu.VMEM((3, cy, cx, cz), F32), pltpu.VMEM((6, cy, cx, cz), F32)),
         in_specs=[pl.BlockSpec(memory_space=pltpu.MemorySpace.HBM)] * 4 + [vmem] * 4 + [pl.BlockSpec(memory_space=pltpu.SMEM)],
         out_specs=(vmem, vmem),
         scratch_shapes=scratch,

time: 44 us -> 41.2 us (0.936)
  Pallas kernels: 40.8 us -> 38.9 us
  local copies, waits for them, and re-layouts: 2.34 us -> 1.38 us
    pallas_call x1, Pallas kernels: 40.8 us -> 38.9 us  [per_device(): pl.pallas_call(functools.partial(body, sizes), out_shape=(pltpu.VMEM((3,...]
    unnamed x4 -> x2, local copies, waits for them, and re-layouts: 2.34 us -> 1.38 us
where the time goes in v3:
time: 41.2 us; the launch traced here: 40.9 us
  Pallas kernels  38.9 us (94%)
  local copies, waits for them, and re-layouts  1.38 us (3%)
  between operations  0.64 us (2%)
    pallas_call x1, Pallas kernels, per_device(): pl.pallas_call(functools.partial(body, sizes), out_shape=(pltpu.VMEM((3,...  38.9 us
    unnamed x2, local copies, waits for them, and re-layouts  1.38 us

profile of v3, /device:TPU:1, one launch (start us, length us, event | category | flops | bytes accessed | tf_op | source)
XLA Modules:
  0.0 40.9 jit_solution(4124768206948465107)
XLA Ops:
  0.6 38.9 %shard_map.95 = (f32[3,12,8,128]{3,2,1,0:T(8,128)S(1)}, f32[6,12,8,128]{3,2,1,0:T(8,128)S(1)}) custom-call(f32[12,8,128]{2,1,0:T(8,128)} %bitcast.14, f32[12,8,128]{2,1,0:T(8,128)} %bitcast.15, f32[3,12,8,128]{3,2,1,0:T(8,128)} %bitcast.13, s32[4,12,8,128]{3,2,1,0:T(8,128)} %bitcast.12, f32[3,16,128]{2,1,0:T(8,128)} %bitcast.16, s32[16,128]{1,0:T(8,128)} %nodes_ref.1, ...), custom_call_target="tpu_custom_call" | custom-call | tf_op jit(solution)/shard_map/pallas_call | solution.py:555
  39.6 0.7 %copy.12 = f32[3,8,12,128]{3,1,2,0:T(8,128)} copy(f32[3,8,12,128]{3,1,2,0:T(8,128)S(1)} %bitcast.11) | data formatting | bytes 294912
  40.2 0.7 %copy.13 = f32[6,8,12,128]{3,1,2,0:T(8,128)} copy(f32[6,8,12,128]{3,1,2,0:T(8,128)S(1)} %bitcast.10) | data formatting | bytes 589824

commit v4 on v3

--- a/solution.py
+++ b/solution.py
@@ -52,9 +52,10 @@
     return jnp.concatenate([-q[:1], q[:-1] - q[1:], q[-1:]], axis=0)
 
 
-def body(sizes, stiff_hbm, dens_hbm, load_hbm, alive_hbm, coords_ref, nodes_ref, routes_ref, pairt_ref, pair_ref,
+def body(sizes, stiff_hbm, dens_hbm, load_hbm, alive_hbm, coords_hbm, nodes_hbm, routes_hbm, pairt_hbm,
          vout_ref, sout_ref, *scratch):
-    (stiff_ref, dens_ref, load_ref, alive_ref, in_sem, mod, big_f, rim_f, load_f, load_r, vel, vel_r, disp, disp_r, minv, minv_r, route_all, pos_all, slots, parts, take_a, turned_b, give_b,
+    (coords_ref, nodes_ref, routes_ref, pairt_ref, pair_ref, early_sem,
+     stiff_ref, dens_ref, load_ref, alive_ref, in_sem, mod, big_f, rim_f, load_f, load_r, vel, vel_r, disp, disp_r, minv, minv_r, route_all, pos_all, slots, parts, take_a, turned_b, give_b,
      partial, send_f, ret, back_pick, choose, pair_hot, rank_in, row_pick, lane_pick, lane_turn, flat, touch, scatter_l,
      x_send, x_recv, y_send, y_recv, edge_send, edge_recv, z_send, z_recv, zx_recv, line_send, line_recv,
      route_ss, route_rs, pos_ss, pos_rs, ret_ss, ret_rs, halo_ss, halo_rs) = scratch
@@ -71,7 +72,9 @@
 
     inputs = [pltpu.make_async_copy(a, b, in_sem.at[k]) for k, (a, b) in enumerate((
         (stiff_hbm, stiff_ref), (alive_hbm, alive_ref), (load_hbm, load_ref), (dens_hbm, dens_ref)))]
-    for c in inputs:
+    tables = [pltpu.make_async_copy(a, b, early_sem.at[k]) for k, (a, b) in enumerate((
+        (coords_hbm, coords_ref), (routes_hbm, routes_ref), (nodes_hbm, nodes_ref), (pairt_hbm, pairt_ref), (pairt_hbm, pair_ref)))]
+    for c in tables + inputs:
         c.start()
 
     def clear(*refs):
@@ -109,6 +112,8 @@
         def _():
             pl.semaphore_signal(barrier, inc=1, device_id={"gz": far}, device_id_type=MESH)
         expect = expect + jnp.where(apart, 1, 0)
+    for c in tables:
+        c.wait()
     pl.semaphore_wait(barrier, expect)
 
     def column(send_ref, recv_ref, ss, rs):
@@ -394,6 +399,27 @@
         for wy, line in lines:
             line_send[t, 0, wy] = packed[line:line + 1]
             line_send[t, 1, wy] = rim_f[line:line + 1]
+        copies = list(zip(ways, halo_copies(t, comps, used), sends, gets))
+        along_z = [m[1:] for m in copies if m[0][2]]
+        in_plane = [m[1:] for m in copies if not m[0][2]]
+
+        def begin(messages):
+            for copy, here, _ in messages:
+                @pl.when(here)
+                def _():
+                    copy.start()
+
+        def end(messages):
+            for copy, here, back in messages:
+                @pl.when(here)
+                def _():
+                    copy.wait_send()
+
+                @pl.when(back)
+                def _():
+                    copy.wait_recv()
+
+        begin(along_z)
         for wx, plane in ((0, 0), (1, cx)):
             x_send[t, wx, 0] = rim_f[...]
             for c in range(comps):
@@ -408,21 +434,9 @@
                 for i in range(nx):
                     at = 1 + c * nx + i
                     y_send[t, wy, at:at + 1] = big_f[c, i, line:line + 1]
-        copies = halo_copies(t, comps, used)
-        for copy, here in zip(copies, sends):
-            @pl.when(here)
-            def _():
-                copy.start()
-
+        begin(in_plane)
         filler()
-        for copy, here, back in zip(copies, sends, gets):
-            @pl.when(here)
-            def _():
-                copy.wait_send()
-
-            @pl.when(back)
-            def _():
-                copy.wait_recv()
+        end(in_plane)
 
         def across(tile, wx):
             at = line_lanes if tile.shape[0] == 1 else lanes
@@ -437,9 +451,7 @@
                 base = base + jnp.where(row_at == line, value, 0.0)
             return base
 
-        folded = [fold(z_recv[t, w], [zx_recv[t, w, wx] for wx in range(2)], [line_recv[t, w, wy, 1] for wy in range(2)],
-                       [[line_recv[t, w, wy, 2 * wx] for wy in range(2)] for wx in range(2)]) for w in range(2)]
-        rim_f[...] = folded[0] + fold(
+        rim_f[...] = fold(
             rim_f[...], [x_recv[t, wx, 0] for wx in range(2)], [y_recv[t, wy, 0:1] for wy in range(2)],
             [[edge_recv[t, wx, wy, 0:1] for wy in range(2)] for wx in range(2)])
         for c in range(comps):
@@ -454,6 +466,11 @@
                         wx = 1 if i == 0 else 0
                         add = add + edge_recv[t, wx, wy, 1 + c:2 + c]
                     big_f[c, i, line:line + 1] = big_f[c, i, line:line + 1] + add
+
+        end(along_z)
+        folded = [fold(z_recv[t, w], [zx_recv[t, w, wx] for wx in range(2)], [line_recv[t, w, wy, 1] for wy in range(2)],
+                       [[line_recv[t, w, wy, 2 * wx] for wy in range(2)] for wx in range(2)]) for w in range(2)]
+        rim_f[...] = rim_f[...] + folded[0]
         for c in range(comps):
             for i in range(nx):
                 at = c * nx + i
@@ -537,6 +554,8 @@
     dma = lambda *shape: pltpu.SemaphoreType.DMA(shape)
     column = max(nz - 1, 1)
     scratch = [
+        vm(3, sb, 128), pltpu.VMEM((sb, 128), jnp.int32), pltpu.VMEM((steps, sb), jnp.int32),
+        pltpu.VMEM((steps, 2, npair), jnp.int32), pltpu.SMEM((steps, 2, npair), jnp.int32), dma(5),
         vm(cy, cx, cz), vm(cy, cx, cz), vm(3, cy, cx, cz), pltpu.VMEM((steps, cy, cx, cz), jnp.int32), dma(4),
         vm(steps + 4, cx, 16, cz), vm(4, nx, 16, cz), vm(16, cz), vm(4, nx, 16, cz), vm(16, cz),
         vm(3, nx, 16, cz), vm(16, cz), vm(3, nx, 16, cz), vm(16, cz), vm(nx, 16, cz), vm(16, cz),
@@ -555,12 +574,12 @@
     vel, stress = pl.pallas_call(
         functools.partial(body, sizes),
         out_shape=(pltpu.VMEM((3, cy, cx, cz), F32), pltpu.VMEM((6, cy, cx, cz), F32)),
-        in_specs=[pl.BlockSpec(memory_space=pltpu.MemorySpace.HBM)] * 4 + [vmem] * 4 + [pl.BlockSpec(memory_space=pltpu.SMEM)],
+        in_specs=[pl.BlockSpec(memory_space=pltpu.MemorySpace.HBM)] * 8,
         out_specs=(vmem, vmem),
         scratch_shapes=scratch,
         compiler_params=pltpu.CompilerParams(collective_id=0, has_side_effects=True, vmem_limit_bytes=56 * 1024 * 1024),
     )(jnp.swapaxes(stiffness, 0, 1), jnp.swapaxes(density, 0, 1), jnp.swapaxes(load, 1, 2), jnp.swapaxes(alive, 1, 2),
-      jnp.swapaxes(surf_coords, 0, 1), surf_nodes, routes, pairt, pairt)
+      jnp.swapaxes(surf_coords, 0, 1), surf_nodes, routes, pairt)
     return jnp.swapaxes(vel, 1, 2), jnp.swapaxes(stress, 1, 2)
 
 

time: 41.2 us -> 40.6 us (0.985)
  Pallas kernels: 38.9 us -> 38.4 us
    pallas_call x1, Pallas kernels: 38.9 us -> 38.4 us  [per_device(): pl.pallas_call(functools.partial(body, sizes), out_shape=(pltpu.VMEM((3,...]
where the time goes in v4:
time: 40.6 us; the launch traced here: 40.4 us
  Pallas kernels  38.4 us (95%)
  local copies, waits for them, and re-layouts  1.38 us (3%)
  between operations  0.64 us (2%)
    pallas_call x1, Pallas kernels, per_device(): pl.pallas_call(functools.partial(body, sizes), out_shape=(pltpu.VMEM((3,...  38.4 us
    unnamed x2, local copies, waits for them, and re-layouts  1.38 us

profile of v4, /device:TPU:1, one launch (start us, length us, event | category | flops | bytes accessed | tf_op | source)
XLA Modules:
  0.0 40.4 jit_solution(16527372108370717697)
XLA Ops:
  0.6 38.4 %shard_map.95 = (f32[3,12,8,128]{3,2,1,0:T(8,128)S(1)}, f32[6,12,8,128]{3,2,1,0:T(8,128)S(1)}) custom-call(f32[12,8,128]{2,1,0:T(8,128)} %bitcast.14, f32[12,8,128]{2,1,0:T(8,128)} %bitcast.15, f32[3,12,8,128]{3,2,1,0:T(8,128)} %bitcast.13, s32[4,12,8,128]{3,2,1,0:T(8,128)} %bitcast.12, f32[3,16,128]{2,1,0:T(8,128)} %bitcast.16, s32[16,128]{1,0:T(8,128)} %nodes_hbm.1, ...), custom_call_target="tpu_custom_call" | custom-call | tf_op jit(solution)/shard_map/pallas_call | solution.py:574
  39.0 0.7 %copy.12 = f32[3,8,12,128]{3,1,2,0:T(8,128)} copy(f32[3,8,12,128]{3,1,2,0:T(8,128)S(1)} %bitcast.11) | data formatting | bytes 294912
  39.7 0.7 %copy.13 = f32[6,8,12,128]{3,1,2,0:T(8,128)} copy(f32[6,8,12,128]{3,1,2,0:T(8,128)S(1)} %bitcast.10) | data formatting | bytes 589824

commit v5 on v4

--- a/solution.py
+++ b/solution.py
@@ -500,8 +500,11 @@
                 gather(t)
                 for c in pos_copies(t):
                     c.start()
-            wait_all(ret_copies(t))
-            internal(t)
+                internal(t)
+                wait_all(ret_copies(t))
+            else:
+                wait_all(ret_copies(t))
+                internal(t)
         scatter(t)
         for c in range(3):
             for i in range(cx):

time: 40.6 us -> 40.5 us (level)
  no operation moved by 1% of the time
where the time goes in v5:
time: 40.5 us; the launch traced here: 40.3 us
  Pallas kernels  38.3 us (95%)
  local copies, waits for them, and re-layouts  1.38 us (3%)
  between operations  0.64 us (2%)
    pallas_call x1, Pallas kernels, per_device(): pl.pallas_call(functools.partial(body, sizes), out_shape=(pltpu.VMEM((3,...  38.3 us
    unnamed x2, local copies, waits for them, and re-layouts  1.38 us

profile of v5, /device:TPU:1, one launch (start us, length us, event | category | flops | bytes accessed | tf_op | source)
XLA Modules:
  0.0 40.3 jit_solution(609968318437708033)
XLA Ops:
  0.6 38.3 %shard_map.95 = (f32[3,12,8,128]{3,2,1,0:T(8,128)S(1)}, f32[6,12,8,128]{3,2,1,0:T(8,128)S(1)}) custom-call(f32[12,8,128]{2,1,0:T(8,128)} %bitcast.14, f32[12,8,128]{2,1,0:T(8,128)} %bitcast.15, f32[3,12,8,128]{3,2,1,0:T(8,128)} %bitcast.13, s32[4,12,8,128]{3,2,1,0:T(8,128)} %bitcast.12, f32[3,16,128]{2,1,0:T(8,128)} %bitcast.16, s32[16,128]{1,0:T(8,128)} %nodes_hbm.1, ...), custom_call_target="tpu_custom_call" | custom-call | tf_op jit(solution)/shard_map/pallas_call | solution.py:577
  39.0 0.7 %copy.12 = f32[3,8,12,128]{3,1,2,0:T(8,128)} copy(f32[3,8,12,128]{3,1,2,0:T(8,128)S(1)} %bitcast.11) | data formatting | bytes 294912
  39.6 0.7 %copy.13 = f32[6,8,12,128]{3,1,2,0:T(8,128)} copy(f32[6,8,12,128]{3,1,2,0:T(8,128)S(1)} %bitcast.10) | data formatting | bytes 589824
